TPU v7x, 256 devices: a whole 4x4x8 slice. The times are simulated.
256 devices in a mesh: row: 8 (over y, core), col: 32 (over z, x).
Axes of the slice: x: 4, y: 4, z: 8, core: 2. Of those that a mesh axis runs over, the one named last changes fastest.
Arguments:
- hidden: bfloat16 [1024, 24576], P(None, 'row'), may hold values from -6 to 6
- down_weight: bfloat16 [24576, 6144], P('row', 'col'), may hold values from -0.0390625 to 0.0390625
- residual: bfloat16 [1024, 6144], P('row', 'col'), may hold values from -260 to 260
- gain: bfloat16 [6144], P('col'), may hold values from 0.099609375 to 1.8984375
- qk_weight: bfloat16 [6144, 12288], P(None, 'col'), may hold values from -0.078125 to 0.078125
Outputs:
- stream: bfloat16 [1024, 6144], P('row', 'col')
- queries_keys: bfloat16 [1024, 12288], P('row', 'col')
All inputs are finite; a program needn't handle non-finite values.
Results may differ from a plain program's by a relative error of at most 0.015.
Values may be sent and summed in bfloat16 or wider, within the bound.
A program may use at most 64 MiB of HBM per device.

v0:
```python
import jax
import jax.numpy as jnp
from jax import lax
from jax.sharding import PartitionSpec as P


def joined(value, axis, join):
    pieces = jax.tree.map(lambda part: lax.all_gather(part, axis), value)
    head = jax.tree.map(lambda part: part[0], pieces)
    tail = jax.tree.map(lambda part: part[1:], pieces)
    total, _ = lax.scan(lambda total, section: (join(total, section), None), head, tail)
    return total


def combine_moments(first, second):
    count_a, mean_a, spread_a = first
    count_b, mean_b, spread_b = second
    count = count_a + count_b
    delta = mean_b - mean_a
    mean = mean_a + delta * count_b / count
    spread = spread_a + spread_b + delta * delta * count_a * count_b / count
    return (count, mean, spread)


def per_device(hidden, down_weight, residual, gain, qk_weight):
    tok_rows = residual.shape[0]
    mlp = lax.psum_scatter(
        jnp.dot(hidden, down_weight, preferred_element_type=jnp.float32).astype(jnp.bfloat16),
        "row",
        scatter_dimension=0,
        tiled=True,
    ).astype(jnp.float32)
    stream = (residual.astype(jnp.float32) + mlp).astype(jnp.bfloat16)
    values = stream.astype(jnp.float32)
    local_width = values.shape[1]
    local_mean = jnp.mean(values, axis=1)
    local_dev = values - local_mean[:, None]
    local_spread = jnp.sum(local_dev * local_dev, axis=1)
    counts = jnp.full((tok_rows,), float(local_width), jnp.float32)
    total_count, mean_flat, spread_flat = joined(
        (counts, local_mean, local_spread), "col", combine_moments
    )
    mean = mean_flat[:, None]
    var = (spread_flat / total_count)[:, None]
    normed = ((values - mean) / jnp.sqrt(var + 1e-06) * gain.astype(jnp.float32)[None, :]).astype(
        jnp.bfloat16
    )
    product = jnp.dot(
        lax.all_gather(normed, "col", axis=1, tiled=True),
        qk_weight,
        preferred_element_type=jnp.float32,
    )
    return (stream, product.astype(jnp.bfloat16))


def solution(mesh):
    placed = (P(None, "row"), P("row", "col"), P("row", "col"), P("col"), P(None, "col"))
    return jax.shard_map(
        per_device,
        mesh=mesh,
        in_specs=placed,
        out_specs=(P("row", "col"), P("row", "col")),
        check_vma=False,
    )
```

profile of v0, /device:TPU:8, one launch (start us, length us, event | category | flops | bytes accessed | tf_op | source)
XLA Modules:
  0.0 214.9 jit_solution(6401340985521224175)
XLA Ops:
  7.2 0.0 copy-start
  7.2 0.0 copy-start.3
  7.2 0.0 copy-start.2
  7.2 0.0 reduce-scatter.4.cloned.1.call-start
  7.2 1.2 copy-done
  8.4 5.0 %convolution_convert_fusion = bf16[1024,192]{0,1:T(8,128)(2,1)S(1)} fusion(bf16[1024,3072]{1,0:T(8,128)(2,1)} %param.7, bf16[3072,192]{0,1:T(8,128)(2,1)S(1)} %copy-done), kind=kOutput, calls=%fused_computation.6 | convolution fusion | flops 1208156160 | bytes 7864320 | tf_op jit(solution)/shard_map/dot_general | solution.py:28
  13.4 1.0 copy.7
  14.4 0.0 reduce-scatter.4.cloned.1.call-update
  14.5 0.0 all-gather.6.cloned.1.call-start
  14.5 0.0 copy-done.3
  14.5 33.4 %reduce-scatter.4.cloned.1.call-done = bf16[128,192]{1,0:T(8,128)(2,1)} async-done(((bf16[1024,192]{1,0:T(8,128)(2,1)}), bf16[128,192]{1,0:T(8,128)(2,1)}) %reduce-scatter.4.cloned.1.call-update) | async-done | bytes 49168
  48.0 0.9 copy.8
  48.9 0.0 copy-done.2
  49.0 0.0 copy-start.1
  49.0 40.2 %all-gather.3 = f32[32,1,128]{2,1,0:T(1,128)S(1)} all-gather(f32[1,1,128]{2,1,0:T(1,128)S(1)} %bitcast.36), channel_id=3, replica_groups=mesh['row'=8,'col'=32] {'col'}, dimensions={0}, use_global_device_ids=true | all-gather | bytes 16896 | tf_op jit(solution)/shard_map/all_gather | solution.py:8
  89.3 36.5 %all-gather.2 = f32[32,1,128]{2,1,0:T(1,128)S(1)} all-gather(f32[1,1,128]{2,1,0:T(1,128)S(1)} %get-tuple-element.100), channel_id=2, replica_groups=mesh['row'=8,'col'=32] {'col'}, dimensions={0}, use_global_device_ids=true | all-gather | bytes 16896 | tf_op jit(solution)/shard_map/all_gather | solution.py:8
  125.8 2.0 while.16
  127.8 0.7 fusion.5
  128.5 0.0 all-gather.6.cloned.1.call-update
  128.5 75.0 %all-gather.6.cloned.1.call-done = bf16[128,6144]{0,1:T(8,128)(2,1)} async-done(((bf16[128,192]{0,1:T(8,128)(2,1)}), bf16[128,6144]{0,1:T(8,128)(2,1)}) %all-gather.6.cloned.1.call-update) | async-done | bytes 1572880 | tf_op jit(solution)/shard_map/all_gather | solution.py:49
  203.5 4.5 %convolution_convert_fusion.1 = bf16[128,384]{1,0:T(8,128)(2,1)} fusion(bf16[128,6144]{0,1:T(8,128)(2,1)} %all-gather.6.cloned.1.call-done, bf16[6144,384]{1,0:T(8,128)(2,1)} %param.11), kind=kOutput, calls=%fused_computation.7 | convolution fusion | flops 604028928 | bytes 6389760 | tf_op jit(solution)/shard_map/dot_general | solution.py:48
  208.0 0.0 copy-done.1
  (74 shorter events, 1.5 us)
Async XLA Ops:
  7.2 1.3 copy-start
  7.2 7.3 %copy-start.3 = (bf16[192]{0:T(256)(128)(2,1)S(1)}, bf16[192]{0:T(256)(128)(2,1)}, u32[]{:S(2)}) copy-start(bf16[192]{0:T(256)(128)(2,1)} %param.10) | copy-start | bytes 1156
  7.2 41.7 %copy-start.2 = (bf16[128,192]{0,1:T(8,128)(2,1)S(1)}, bf16[128,192]{0,1:T(8,128)(2,1)}, u32[]{:S(2)}) copy-start(bf16[128,192]{0,1:T(8,128)(2,1)} %param.9) | copy-start | bytes 147460
  7.2 40.8 %reduce-scatter.4.cloned.1.call-start = ((), (), s32[]{:S(2)}) async-start(), calls=%async_computation.2 | async-start | bytes 589824
  14.5 189.1 %all-gather.6.cloned.1.call-start = ((), (), s32[]{:S(2)}) async-start(), calls=%async_computation.1 | async-start | bytes 1622016 | tf_op jit(solution)/shard_map/all_gather | solution.py:49
  49.0 159.0 %copy-start.1 = (bf16[128,192]{0,1:T(8,128)(2,1)}, bf16[128,192]{0,1:T(8,128)(2,1)S(1)}, u32[]{:S(2)}) copy-start(bf16[128,192]{0,1:T(8,128)(2,1)S(1)} %get-tuple-element.98) | copy-start | bytes 147460
Sparse Core Ops, SparseCore 0:
  14.6 33.3 reduce-scatter.3
  128.6 74.8 all-gather.5
where the time goes:
time: 215 us
  waiting for transfers between devices  108 us (50%)
  blocking collectives  76.7 us (36%)
  between operations  14.1 us (7%)
  matrix products  9.48 us (4%)
  local copies, waits for them, and re-layouts  3.16 us (1%)
  other arithmetic  2.24 us (1%)
    all_gather x2, blocking collectives, joined(): pieces = jax.tree.map(lambda part: lax.all_gather(part, axis), value)  76.7 us
    all_gather x1, waiting for transfers between devices, per_device(): lax.all_gather(normed, 'col', axis=1, tiled=True)  75 us
    unnamed x3, waiting for transfers between devices  33.5 us
    dot_general x1, matrix products, per_device(): jnp.dot(hidden, down_weight, preferred_element_type=jnp.float32)  4.99 us
    dot_general x1, matrix products, per_device(): jnp.dot(lax.all_gather(normed, 'col', axis=1, tiled=True), qk_weight, pre...  4.49 us
  transfers between devices with their start and end apart: 2, of which 2 were waited for; matrix products, arithmetic and copies ran while one was open for 0% of the time, Pallas kernels for 0%

commit v1 on v0

--- a/solution.py
+++ b/solution.py
@@ -46,7 +46,15 @@
         jnp.bfloat16
     )
     product = jnp.dot(
-        lax.all_gather(normed, "col", axis=1, tiled=True),
+        jnp.concatenate(
+            jax.lax.all_to_all(
+                jnp.stack([normed for _ in range(jax.lax.axis_size("col"))], axis=0),
+                split_axis=0,
+                concat_axis=0,
+                axis_name="col",
+            ),
+            1,
+        ),
         qk_weight,
         preferred_element_type=jnp.float32,
     )

time: 215 us -> 173 us (0.80)
  the two profiles are of different devices: /device:TPU:8 before, /device:TPU:2 now
where the time goes in v1:
time: 173 us
  blocking collectives  110 us (64%)
  waiting for transfers between devices  36.6 us (21%)
  between operations  14.2 us (8%)
  matrix products  6.65 us (4%)
  local copies, waits for them, and re-layouts  3.53 us (2%)
    all_gather x2, blocking collectives, joined(): pieces = jax.tree.map(lambda part: lax.all_gather(part, axis), value)  77.5 us
    unnamed x2, waiting for transfers between devices  36.6 us
    all_to_all x1, blocking collectives, per_device(): jax.lax.all_to_all(jnp.stack([normed for _ in range(jax.lax.axis_size('co...  32.4 us
    dot_general x1, matrix products, per_device(): jnp.dot(hidden, down_weight, preferred_element_type=jnp.float32)  4.99 us
  transfers between devices with their start and end apart: 1, of which 1 were waited for; matrix products, arithmetic and copies ran while one was open for 0% of the time, Pallas kernels for 0%

profile of v1, /device:TPU:2, one launch (start us, length us, event | category | flops | bytes accessed | tf_op | source)
XLA Modules:
  0.0 173.0 jit_solution(764822216549478981)
XLA Ops:
  7.2 0.0 copy-start
  7.2 0.0 copy-start.4
  7.2 0.0 reduce-scatter.4.cloned.1.call-start
  7.2 1.2 copy-done
  8.4 5.0 %convolution_convert_fusion = bf16[1024,192]{0,1:T(8,128)(2,1)S(1)} fusion(bf16[1024,3072]{1,0:T(8,128)(2,1)} %param.7, bf16[3072,192]{0,1:T(8,128)(2,1)S(1)} %copy-done), kind=kOutput, calls=%fused_computation.6 | convolution fusion | flops 1208156160 | bytes 7864320 | tf_op jit(solution)/shard_map/dot_general | solution.py:28
  13.4 0.0 copy-start.3
  13.4 1.0 copy.8
  14.4 0.0 reduce-scatter.4.cloned.1.call-update
  14.5 0.0 copy-done.4
  14.5 36.6 %reduce-scatter.4.cloned.1.call-done = bf16[128,192]{1,0:T(8,128)(2,1)} async-done(((bf16[1024,192]{1,0:T(8,128)(2,1)}), bf16[128,192]{1,0:T(8,128)(2,1)}) %reduce-scatter.4.cloned.1.call-update) | async-done | bytes 49168
  51.1 0.9 copy.9
  52.0 0.0 copy-done.3
  52.1 0.0 copy-start.2
  52.1 39.9 %all-gather.3 = f32[32,1,128]{2,1,0:T(1,128)S(1)} all-gather(f32[1,1,128]{2,1,0:T(1,128)S(1)} %bitcast.40), channel_id=3, replica_groups=mesh['row'=8,'col'=32] {'col'}, dimensions={0}, use_global_device_ids=true | all-gather | bytes 16896 | tf_op jit(solution)/shard_map/all_gather | solution.py:8
  92.0 37.6 %all-gather.2 = f32[32,1,128]{2,1,0:T(1,128)S(1)} all-gather(f32[1,1,128]{2,1,0:T(1,128)S(1)} %get-tuple-element.100), channel_id=2, replica_groups=mesh['row'=8,'col'=32] {'col'}, dimensions={0}, use_global_device_ids=true | all-gather | bytes 16896 | tf_op jit(solution)/shard_map/all_gather | solution.py:8
  129.7 2.0 %while.16 = (s32[]{:T(128)}, f32[128]{0:T(128)S(1)}, f32[128]{0:T(128)S(1)}, f32[128]{0:T(128)S(1)}, f32[31,128]{1,0:T(8,128)S(1)}, /*index=5*/f32[31,128]{1,0:T(8,128)S(1)}, s32[]{:T(128)}, s32[]{:T(128)}) while((s32[]{:T(128)}, f32[128]{0:T(128)S(1)}, f32[128]{0:T(128)S(1)}, f32[128]{0:T(128)S(1)}, f32[31,128]{1,0:T(8,128)S(1)}, ...), condition=%wide.region_4.5_spmd.clone, body=%wide.region_3.4_spmd.clone.sunk | while | flops 1667 | bytes 5743 | solution.py:11
  131.7 0.1 fusion.5
  131.8 0.0 copy-start.1
  131.8 0.3 stack.2
  132.1 32.4 %all_to_all.5 = bf16[32,128,192]{1,2,0:T(8,128)(2,1)S(1)} all-to-all(bf16[32,128,192]{1,2,0:T(8,128)(2,1)S(1)} %stack.2), channel_id=1, replica_groups=mesh['row'=8,'col'=32] {'col'}, dimensions={0} | all-to-all | bytes 3145728 | tf_op jit(solution)/shard_map/all_to_all | solution.py:50
  164.5 0.0 copy-done.2
  164.5 0.0 copy-done.1
  164.5 1.7 convolution_convert_fusion.1
  (74 shorter events, 1.5 us)
Async XLA Ops:
  7.2 1.3 copy-start
  7.2 7.3 %copy-start.4 = (bf16[192]{0:T(256)(128)(2,1)S(1)}, bf16[192]{0:T(256)(128)(2,1)}, u32[]{:S(2)}) copy-start(bf16[192]{0:T(256)(128)(2,1)} %param.10) | copy-start | bytes 1156
  7.2 43.9 %reduce-scatter.4.cloned.1.call-start = ((), (), s32[]{:S(2)}) async-start(), calls=%async_computation.2 | async-start | bytes 589824
  13.4 38.6 %copy-start.3 = (bf16[128,192]{0,1:T(8,128)(2,1)S(1)}, bf16[128,192]{0,1:T(8,128)(2,1)}, u32[]{:S(2)}) copy-start(bf16[128,192]{0,1:T(8,128)(2,1)} %param.9) | copy-start | bytes 147460
  52.1 112.4 %copy-start.2 = (bf16[128,192]{0,1:T(8,128)(2,1)}, bf16[128,192]{0,1:T(8,128)(2,1)S(1)}, u32[]{:S(2)}) copy-start(bf16[128,192]{0,1:T(8,128)(2,1)S(1)} %get-tuple-element.98) | copy-start | bytes 147460
  131.8 32.7 %copy-start.1 = (bf16[6144,384]{1,0:T(8,128)(2,1)S(1)}, bf16[6144,384]{1,0:T(8,128)(2,1)}, u32[]{:S(2)}) copy-start(bf16[6144,384]{1,0:T(8,128)(2,1)} %param.11) | copy-start | bytes 14155780
Sparse Core Ops, SparseCore 0:
  14.6 36.4 reduce-scatter.3
